TPU v7x, 128 devices: a whole 4x4x4 slice. The times are simulated.
128 devices in a mesh: dp: 16 (over y, z), fsdp: 8 (over x, core).
Axes of the slice: x: 4, y: 4, z: 4, core: 2. Of those that a mesh axis runs over, the one named last changes fastest.
Arguments:
- tokens: bfloat16 [128, 8, 64, 768], P(('dp', 'fsdp')), may hold values from -6 to 6
- cotangent: bfloat16 [128, 8, 64, 768], P(('dp', 'fsdp')), may hold values from -6 to 6
- lengths: int32 [128], P(('dp', 'fsdp')), may hold values from 32 to 64
- row_offset: int32 [128], P(('dp', 'fsdp')), may hold values from 0 to 1016
- col_offset: int32 [128], P(('dp', 'fsdp')), may hold values from 0 to 960
- norm_gain: bfloat16 [3, 768], P(None, ('dp', 'fsdp')), may hold values from 0.099609375 to 1.8984375
- norm_bias: bfloat16 [3, 768], P(None, ('dp', 'fsdp')), may hold values from -1.75 to 1.75
- row_qkv: bfloat16 [3, 768, 768], P(None, ('dp', 'fsdp')), may hold values from -0.21875 to 0.21875
- row_out: bfloat16 [768, 768], P(('dp', 'fsdp')), may hold values from -1.25 to 1.25
- row_bias: bfloat16 [3, 768], P(None, ('dp', 'fsdp')), may hold values from -1.75 to 1.75
- col_qkv: bfloat16 [3, 768, 768], P(None, ('dp', 'fsdp')), may hold values from -0.21875 to 0.21875
- col_out: bfloat16 [768, 768], P(('dp', 'fsdp')), may hold values from -0.4375 to 0.4375
- col_bias: bfloat16 [3, 768], P(None, ('dp', 'fsdp')), may hold values from -1.75 to 1.75
- ffn_up: bfloat16 [768, 3072], P(('dp', 'fsdp')), may hold values from -0.21875 to 0.21875
- up_bias: bfloat16 [3072], P(('dp', 'fsdp')), may hold values from -1.75 to 1.75
- ffn_down: bfloat16 [3072, 768], P(('dp', 'fsdp')), may hold values from -0.15625 to 0.15625
- down_bias: bfloat16 [768], P(('dp', 'fsdp')), may hold values from -1.75 to 1.75
- pos_tables: bfloat16 [2, 1024, 768], P(None, ('dp', 'fsdp')), may hold values from -3 to 3
Outputs:
- activations: bfloat16 [128, 8, 64, 768], P(('dp', 'fsdp'))
- tokens_grad: float32 [128, 8, 64, 768], P(('dp', 'fsdp'))
- norm_gain_grad: float32 [3, 768], P(None, ('dp', 'fsdp'))
- norm_bias_grad: float32 [3, 768], P(None, ('dp', 'fsdp'))
- row_qkv_grad: float32 [3, 768, 768], P(None, ('dp', 'fsdp'))
- row_out_grad: float32 [768, 768], P(('dp', 'fsdp'))
- row_bias_grad: float32 [3, 768], P(None, ('dp', 'fsdp'))
- col_qkv_grad: float32 [3, 768, 768], P(None, ('dp', 'fsdp'))
- col_out_grad: float32 [768, 768], P(('dp', 'fsdp'))
- col_bias_grad: float32 [3, 768], P(None, ('dp', 'fsdp'))
- ffn_up_grad: float32 [768, 3072], P(('dp', 'fsdp'))
- up_bias_grad: float32 [3072], P(('dp', 'fsdp'))
- ffn_down_grad: float32 [3072, 768], P(('dp', 'fsdp'))
- down_bias_grad: float32 [768], P(('dp', 'fsdp'))
- pos_tables_grad: float32 [2, 1024, 768], P(None, ('dp', 'fsdp'))
All inputs are finite; a program needn't handle non-finite values.
Results may differ from a plain program's by a relative error of at most 0.018.
Values may be sent and summed in bfloat16 or wider, within the bound.
No kernel may reach another device: no remote copies, remote signals or barrier semaphores. Data moves between devices by JAX's collectives and lax.ppermute only.
A program may use at most 256 MiB of HBM per device.

v0:
```python
import math

import jax
import jax.numpy as jnp
from jax import lax
from jax.sharding import PartitionSpec as P

HEADS = 12
HEAD_DIM = 64
POSITIONS = 1024


eps = 1e-05
row_forms = ("rihe,rjhe->hij", "hij,rjhe->rihe", "hij,rihe->rjhe")
col_forms = ("rche,tche->chrt", "chrt,tche->rche", "chrt,rche->tche")


def product(left_arr, right_arr):
    return jnp.dot(left_arr, right_arr, preferred_element_type=jnp.float32)


def product_t(left_arr, right_arr):
    return lax.dot_general(
        left_arr, right_arr, (((0,), (0,)), ((), ())), preferred_element_type=jnp.float32
    )


def product_nt(left_arr, right_arr):
    return lax.dot_general(
        left_arr, right_arr, (((1,), (1,)), ((), ())), preferred_element_type=jnp.float32
    )


def rounded(value):
    return lax.optimization_barrier(value.astype(jnp.bfloat16)).astype(jnp.float32)


def gelu_exact(value):
    return jax.nn.gelu(value, approximate=False)


def norm_forward(hidden, gain_vec, shift_vec):
    centred = hidden - jnp.mean(hidden, axis=-1, keepdims=True)
    inverse = lax.rsqrt(jnp.mean(centred * centred, axis=-1, keepdims=True) + eps)
    unit_value = centred * inverse
    return (unit_value * gain_vec + shift_vec, unit_value, inverse)


def norm_backward(grad_norm, unit_value, inverse, gain_vec):
    grad_unit = grad_norm * gain_vec
    grad_in = inverse * (
        grad_unit
        - jnp.mean(grad_unit, axis=-1, keepdims=True)
        - unit_value * jnp.mean(grad_unit * unit_value, axis=-1, keepdims=True)
    )
    return (grad_in, jnp.sum(grad_norm * unit_value, axis=0), jnp.sum(grad_norm, axis=0))


def attend(normed, projection, out_proj, biases, shape_heads, score_scale, key_mask, einsum_forms):
    queries = (product(normed, projection[0]) + biases[0]).astype(jnp.bfloat16).reshape(shape_heads)
    key_act = product(normed, projection[1]).astype(jnp.bfloat16).reshape(shape_heads)
    value_act = (
        (product(normed, projection[2]) + biases[1]).astype(jnp.bfloat16).reshape(shape_heads)
    )
    scores = (
        jnp.einsum(einsum_forms[0], queries, key_act, preferred_element_type=jnp.float32)
        * score_scale
    )
    if key_mask is not None:
        scores = jnp.where(key_mask, scores, -1e30)
    softmax_out = jax.nn.softmax(scores, axis=-1)
    softmax_low = softmax_out.astype(jnp.bfloat16)
    mixed_heads = jnp.einsum(
        einsum_forms[1], softmax_low, value_act, preferred_element_type=jnp.float32
    )
    mixed_heads = mixed_heads.astype(jnp.bfloat16).reshape(normed.shape)
    branch = product(mixed_heads, out_proj) + biases[2]
    return (branch, (queries, key_act, value_act, softmax_out, softmax_low, mixed_heads))


def attend_back(grad_branch, normed, projection, out_proj, saved_state, score_scale, einsum_forms):
    queries, key_act, value_act, softmax_out, softmax_low, mixed_heads = saved_state
    grad_low = grad_branch.astype(jnp.bfloat16)
    out_grad = product_t(mixed_heads, grad_low)
    grad_mixed = product_nt(grad_low, out_proj).astype(jnp.bfloat16).reshape(queries.shape)
    grad_soft = jnp.einsum(
        einsum_forms[0], grad_mixed, value_act, preferred_element_type=jnp.float32
    )
    grad_value = jnp.einsum(
        einsum_forms[2], softmax_low, grad_mixed, preferred_element_type=jnp.float32
    )
    grad_value = grad_value.astype(jnp.bfloat16).reshape(normed.shape)
    grad_scores = softmax_out * (
        grad_soft - jnp.sum(grad_soft * softmax_out, axis=-1, keepdims=True)
    )
    grad_scores = grad_scores.astype(jnp.bfloat16)
    grad_query = (
        jnp.einsum(einsum_forms[1], grad_scores, key_act, preferred_element_type=jnp.float32)
        * score_scale
    )
    grad_query = grad_query.astype(jnp.bfloat16).reshape(normed.shape)
    grad_key = (
        jnp.einsum(einsum_forms[2], grad_scores, queries, preferred_element_type=jnp.float32)
        * score_scale
    )
    grad_key = grad_key.astype(jnp.bfloat16).reshape(normed.shape)
    proj_grad = jnp.stack(
        [product_t(normed, grad_query), product_t(normed, grad_key), product_t(normed, grad_value)]
    )
    bias_grad = jnp.stack(
        [
            jnp.sum(grad_query.astype(jnp.float32), axis=0),
            jnp.sum(grad_value.astype(jnp.float32), axis=0),
            jnp.sum(grad_low.astype(jnp.float32), axis=0),
        ]
    )
    grad_normed = (
        product_nt(grad_query, projection[0])
        + product_nt(grad_key, projection[1])
        + product_nt(grad_value, projection[2])
    )
    return (grad_normed, proj_grad, out_grad, bias_grad)


def on_device(
    tokens,
    cotangent,
    lengths,
    row_offset,
    col_offset,
    norm_gain,
    norm_bias,
    row_qkv,
    row_out,
    row_bias,
    col_qkv,
    col_out,
    col_bias,
    ffn_up,
    up_bias,
    ffn_down,
    down_bias,
    pos_tables,
):
    row_count, col_count, model_width = (tokens.shape[1], tokens.shape[2], tokens.shape[3])
    token_count = row_count * col_count
    shape_heads = (row_count, col_count, HEADS, HEAD_DIM)
    row_scale = 1.0 / math.sqrt(HEAD_DIM * row_count)
    col_scale = 1.0 / math.sqrt(HEAD_DIM)
    (
        norm_gains,
        norm_shifts,
        row_proj,
        row_output,
        row_biases,
        col_proj,
        col_output,
        col_biases,
        up_weight,
        up_biases,
        down_weight,
        down_biases,
        tables,
    ) = (
        lax.all_gather(norm_gain, ("dp", "fsdp"), axis=1, tiled=True),
        lax.all_gather(norm_bias, ("dp", "fsdp"), axis=1, tiled=True),
        lax.all_gather(row_qkv, ("dp", "fsdp"), axis=1, tiled=True),
        lax.all_gather(row_out, ("dp", "fsdp"), axis=0, tiled=True),
        lax.all_gather(row_bias, ("dp", "fsdp"), axis=1, tiled=True),
        lax.all_gather(col_qkv, ("dp", "fsdp"), axis=1, tiled=True),
        lax.all_gather(col_out, ("dp", "fsdp"), axis=0, tiled=True),
        lax.all_gather(col_bias, ("dp", "fsdp"), axis=1, tiled=True),
        lax.all_gather(ffn_up, ("dp", "fsdp"), axis=0, tiled=True),
        lax.all_gather(up_bias, ("dp", "fsdp"), axis=0, tiled=True),
        lax.all_gather(ffn_down, ("dp", "fsdp"), axis=0, tiled=True),
        lax.all_gather(down_bias, ("dp", "fsdp"), axis=0, tiled=True),
        lax.all_gather(pos_tables, ("dp", "fsdp"), axis=1, tiled=True),
    )
    gain_rows = norm_gains.astype(jnp.float32)
    shift_rows = norm_shifts.astype(jnp.float32)
    key_mask = jnp.arange(col_count)[None, None, :] < lengths[0]
    valid_cols = (jnp.arange(col_count) < lengths[0]).astype(jnp.float32)
    token_start = tokens[0].astype(jnp.float32)
    row_pos = lax.dynamic_slice_in_dim(tables[0], row_offset[0], row_count, 0).astype(jnp.float32)
    col_pos = lax.dynamic_slice_in_dim(tables[1], col_offset[0], col_count, 0).astype(jnp.float32)
    hidden_in = (token_start + row_pos[:, None, :] + col_pos[None, :, :]).reshape(
        token_count, model_width
    )
    normed_one, unit_one, inverse_one = norm_forward(hidden_in, gain_rows[0], shift_rows[0])
    normed_one = normed_one.astype(jnp.bfloat16)
    row_branch, row_saved = attend(
        normed_one, row_proj, row_output, row_biases, shape_heads, row_scale, key_mask, row_forms
    )
    hidden_mid = hidden_in + row_branch
    normed_two, unit_two, inverse_two = norm_forward(hidden_mid, gain_rows[1], shift_rows[1])
    normed_two = normed_two.astype(jnp.bfloat16)
    col_branch, col_saved = attend(
        normed_two, col_proj, col_output, col_biases, shape_heads, col_scale, None, col_forms
    )
    hidden_late = hidden_mid + col_branch
    normed_three, unit_three, inverse_three = norm_forward(hidden_late, gain_rows[2], shift_rows[2])
    normed_three = normed_three.astype(jnp.bfloat16)
    pre_act = product(normed_three, up_weight) + up_biases
    act_value, gelu_back = jax.vjp(gelu_exact, pre_act)
    act_low = act_value.astype(jnp.bfloat16)
    hidden_out = hidden_late + product(act_low, down_weight) + down_biases
    activations = hidden_out.reshape(tokens.shape).astype(jnp.bfloat16)
    (
        norm_gains,
        norm_shifts,
        row_proj,
        row_output,
        row_biases,
        col_proj,
        col_output,
        col_biases,
        up_weight,
        up_biases,
        down_weight,
        down_biases,
        tables,
    ) = (
        lax.all_gather(norm_gain, ("dp", "fsdp"), axis=1, tiled=True),
        lax.all_gather(norm_bias, ("dp", "fsdp"), axis=1, tiled=True),
        lax.all_gather(row_qkv, ("dp", "fsdp"), axis=1, tiled=True),
        lax.all_gather(row_out, ("dp", "fsdp"), axis=0, tiled=True),
        lax.all_gather(row_bias, ("dp", "fsdp"), axis=1, tiled=True),
        lax.all_gather(col_qkv, ("dp", "fsdp"), axis=1, tiled=True),
        lax.all_gather(col_out, ("dp", "fsdp"), axis=0, tiled=True),
        lax.all_gather(col_bias, ("dp", "fsdp"), axis=1, tiled=True),
        lax.all_gather(ffn_up, ("dp", "fsdp"), axis=0, tiled=True),
        lax.all_gather(up_bias, ("dp", "fsdp"), axis=0, tiled=True),
        lax.all_gather(ffn_down, ("dp", "fsdp"), axis=0, tiled=True),
        lax.all_gather(down_bias, ("dp", "fsdp"), axis=0, tiled=True),
        lax.all_gather(pos_tables, ("dp", "fsdp"), axis=1, tiled=True),
    )
    gain_rows = norm_gains.astype(jnp.float32)
    grad_out = (cotangent[0].astype(jnp.float32) * valid_cols[None, :, None]).reshape(
        token_count, model_width
    )
    grad_low = grad_out.astype(jnp.bfloat16)
    down_grad = product_t(act_low, grad_low)
    down_bias_grad = jnp.sum(grad_low.astype(jnp.float32), axis=0)
    grad_act = rounded(product_nt(grad_low, down_weight))
    grad_pre = gelu_back(grad_act)[0].astype(jnp.bfloat16)
    up_grad = product_t(normed_three, grad_pre)
    up_bias_grad = jnp.sum(grad_pre.astype(jnp.float32), axis=0)
    grad_in_three, gain_grad_three, shift_grad_three = norm_backward(
        product_nt(grad_pre, up_weight), unit_three, inverse_three, gain_rows[2]
    )
    grad_late = grad_out + grad_in_three
    grad_col_normed, col_proj_grad, col_output_grad, col_bias_grad = attend_back(
        grad_late, normed_two, col_proj, col_output, col_saved, col_scale, col_forms
    )
    grad_in_two, gain_grad_two, shift_grad_two = norm_backward(
        grad_col_normed, unit_two, inverse_two, gain_rows[1]
    )
    grad_mid = grad_late + grad_in_two
    grad_row_normed, row_proj_grad, row_output_grad, row_bias_grad = attend_back(
        grad_mid, normed_one, row_proj, row_output, row_saved, row_scale, row_forms
    )
    grad_in_one, gain_grad_one, shift_grad_one = norm_backward(
        grad_row_normed, unit_one, inverse_one, gain_rows[0]
    )
    grad_input = grad_mid + grad_in_one
    grid_grad = grad_input.reshape(row_count, col_count, model_width)
    zero_table = jnp.zeros((POSITIONS, model_width), jnp.float32)
    table_grad = jnp.stack(
        [
            lax.dynamic_update_slice_in_dim(
                zero_table, jnp.sum(grid_grad, axis=1), row_offset[0], 0
            ),
            lax.dynamic_update_slice_in_dim(
                zero_table, jnp.sum(grid_grad, axis=0), col_offset[0], 0
            ),
        ]
    )
    gain_grad = jnp.stack([gain_grad_one, gain_grad_two, gain_grad_three])
    shift_grad = jnp.stack([shift_grad_one, shift_grad_two, shift_grad_three])
    (
        gain_grad,
        shift_grad,
        row_proj_grad,
        row_output_grad,
        row_bias_grad,
        col_proj_grad,
        col_output_grad,
        col_bias_grad,
        up_grad,
        up_bias_grad,
        down_grad,
        down_bias_grad,
        table_grad,
    ) = (
        lax.psum_scatter(gain_grad, ("dp", "fsdp"), scatter_dimension=1, tiled=True),
        lax.psum_scatter(shift_grad, ("dp", "fsdp"), scatter_dimension=1, tiled=True),
        lax.psum_scatter(row_proj_grad, ("dp", "fsdp"), scatter_dimension=1, tiled=True),
        lax.psum_scatter(row_output_grad, ("dp", "fsdp"), scatter_dimension=0, tiled=True),
        lax.psum_scatter(row_bias_grad, ("dp", "fsdp"), scatter_dimension=1, tiled=True),
        lax.psum_scatter(col_proj_grad, ("dp", "fsdp"), scatter_dimension=1, tiled=True),
        lax.psum_scatter(col_output_grad, ("dp", "fsdp"), scatter_dimension=0, tiled=True),
        lax.psum_scatter(col_bias_grad, ("dp", "fsdp"), scatter_dimension=1, tiled=True),
        lax.psum_scatter(up_grad, ("dp", "fsdp"), scatter_dimension=0, tiled=True),
        lax.psum_scatter(up_bias_grad, ("dp", "fsdp"), scatter_dimension=0, tiled=True),
        lax.psum_scatter(down_grad, ("dp", "fsdp"), scatter_dimension=0, tiled=True),
        lax.psum_scatter(down_bias_grad, ("dp", "fsdp"), scatter_dimension=0, tiled=True),
        lax.psum_scatter(table_grad, ("dp", "fsdp"), scatter_dimension=1, tiled=True),
    )
    tokens_grad = grad_input.reshape(tokens.shape)
    return (
        activations,
        tokens_grad,
        gain_grad,
        shift_grad,
        row_proj_grad,
        row_output_grad,
        row_bias_grad,
        col_proj_grad,
        col_output_grad,
        col_bias_grad,
        up_grad,
        up_bias_grad,
        down_grad,
        down_bias_grad,
        table_grad,
    )


def solution(mesh):
    in_specs = (
        P(("dp", "fsdp"), None, None, None),
        P(("dp", "fsdp"), None, None, None),
        P(("dp", "fsdp")),
        P(("dp", "fsdp")),
        P(("dp", "fsdp")),
        P(None, ("dp", "fsdp")),
        P(None, ("dp", "fsdp")),
        P(None, ("dp", "fsdp"), None),
        P(("dp", "fsdp"), None),
        P(None, ("dp", "fsdp")),
        P(None, ("dp", "fsdp"), None),
        P(("dp", "fsdp"), None),
        P(None, ("dp", "fsdp")),
        P(("dp", "fsdp"), None),
        P(("dp", "fsdp")),
        P(("dp", "fsdp"), None),
        P(("dp", "fsdp")),
        P(None, ("dp", "fsdp"), None),
    )
    out_specs = (
        P(("dp", "fsdp"), None, None, None),
        P(("dp", "fsdp"), None, None, None),
        P(None, ("dp", "fsdp")),
        P(None, ("dp", "fsdp")),
        P(None, ("dp", "fsdp"), None),
        P(("dp", "fsdp"), None),
        P(None, ("dp", "fsdp")),
        P(None, ("dp", "fsdp"), None),
        P(("dp", "fsdp"), None),
        P(None, ("dp", "fsdp")),
        P(("dp", "fsdp"), None),
        P(("dp", "fsdp")),
        P(("dp", "fsdp"), None),
        P(("dp", "fsdp")),
        P(None, ("dp", "fsdp"), None),
    )
    return jax.shard_map(
        on_device, mesh=mesh, in_specs=in_specs, out_specs=out_specs, check_vma=False
    )
```

profile of v0, /device:TPU:24, one launch (start us, length us, event | category | flops | bytes accessed | tf_op | source)
XLA Modules:
  0.0 1448.2 jit_solution(5632950593917508892)
XLA Ops:
  15.1 36.8 %all-gather = bf16[128,6,3]{1,2,0:T(4,128)(2,1)S(1)} all-gather(bf16[1,6,3]{1,2,0:T(4,128)(2,1)} %bitcast.302), channel_id=1, replica_groups=mesh['dp'=16,'fsdp'=8] {'dp','fsdp'}, dimensions={0}, use_global_device_ids=true | all-gather | bytes 4644 | tf_op jit(solution)/shard_map/all_gather | solution.py:165
  52.9 33.1 %all-gather.1 = bf16[128,6,3]{1,2,0:T(4,128)(2,1)S(1)} all-gather(bf16[1,6,3]{1,2,0:T(4,128)(2,1)} %bitcast.303), channel_id=1, replica_groups=mesh['dp'=16,'fsdp'=8] {'dp','fsdp'}, dimensions={0}, use_global_device_ids=true | all-gather | bytes 4644 | tf_op jit(solution)/shard_map/all_gather | solution.py:166
  87.1 33.2 %all-gather.2 = bf16[128,6,3]{1,2,0:T(4,128)(2,1)S(1)} all-gather(bf16[1,6,3]{1,2,0:T(4,128)(2,1)S(1)} %bitcast.304), channel_id=1, replica_groups=mesh['dp'=16,'fsdp'=8] {'dp','fsdp'}, dimensions={0}, use_global_device_ids=true | all-gather | bytes 4644 | tf_op jit(solution)/shard_map/all_gather | solution.py:169
  122.2 33.1 %all-gather.4 = bf16[128,6,3]{1,2,0:T(4,128)(2,1)S(1)} all-gather(bf16[1,6,3]{1,2,0:T(4,128)(2,1)S(1)} %bitcast.305), channel_id=1, replica_groups=mesh['dp'=16,'fsdp'=8] {'dp','fsdp'}, dimensions={0}, use_global_device_ids=true | all-gather | bytes 4644 | tf_op jit(solution)/shard_map/all_gather | solution.py:172
  156.7 63.6 %all-reduce.18 = (bf16[3072]{0:T(1024)(128)(2,1)S(1)}, bf16[768]{0:T(1024)(128)(2,1)}) all-reduce(bf16[3072]{0:T(1024)(128)(2,1)S(1)} %dynamic-update-slice, bf16[768]{0:T(1024)(128)(2,1)S(1)} %dynamic-update-slice.1), channel_id=1, replica_groups=mesh['dp'=16,'fsdp'=8] {'dp','fsdp'}, use_global_device_ids=true, to_apply=%add | all-reduce | flops 3840 | bytes 15360
  233.2 41.3 %all-gather.17.cloned.1.call-done = bf16[3,768,768]{2,0,1:T(4,128)(2,1)} async-done(((bf16[3,6,768]{2,0,1:T(4,128)(2,1)}), bf16[3,768,768]{2,0,1:T(4,128)(2,1)}) %all-gather.17.cloned.1.call-update) | async-done | bytes 3538960 | tf_op jit(solution)/shard_map/all_gather | solution.py:167
  274.5 12.3 fusion.94
  323.6 19.0 %all-gather.19.cloned.1.call-done = bf16[3,768,768]{2,0,1:T(4,128)(2,1)} async-done(((bf16[3,6,768]{2,0,1:T(4,128)(2,1)}), bf16[3,768,768]{2,0,1:T(4,128)(2,1)}) %all-gather.19.cloned.1.call-update) | async-done | bytes 3538960 | tf_op jit(solution)/shard_map/all_gather | solution.py:170
  342.5 12.3 fusion.93
  373.0 22.4 %fusion.98 = (f32[64,12,8]{2,1,0:T(8,128)S(1)}, f32[64,12,8,8]{2,3,1,0:T(8,128)S(1)}) fusion(f32[64,12,8,8]{2,3,1,0:T(8,128)S(1)} %fusion.50), kind=kOutput, calls=%fused_computation.221 | output fusion | flops 196615 | bytes 417792 | tf_op jit(solution)/shard_map/sub | solution.py:71
  410.0 6.9 convolution_convert_fusion
  416.9 62.1 %all-gather.27.cloned.1.call-done = bf16[128,6,3072]{2,1,0:T(8,128)(2,1)} async-done(((bf16[1,6,3072]{2,1,0:T(8,128)(2,1)}), bf16[128,6,3072]{2,1,0:T(8,128)(2,1)}) %all-gather.27.cloned.1.call-update) | async-done | bytes 4718608 | tf_op jit(solution)/shard_map/all_gather | solution.py:173
  479.0 7.7 reshape.826
  486.8 22.2 %convert_reduce_fusion = (f32[3072]{0:T(1024)}, bf16[512,3072]{1,0:T(8,128)(2,1)S(1)}, f32[512,3072]{1,0:T(8,128)}, f32[512,3072]{1,0:T(8,128)}) fusion(bf16[512,3072]{1,0:T(8,128)(2,1)} %convolution_convert_fusion, f32[3072]{0:T(1024)} %convert_element_type.308, bf16[768,3072]{1,0:T(8,128)(2,1)} %reshape.826, f32[512,768]{1,0:T(8,128)S(1)} %get-tuple-element.79, ...), kind=kOutput, calls=%fused_computation.17 | convolution fusion | flops 2537419776 | bytes 25200640 | tf_op jit(solution)/shard_map/dot_general | solution.py:19
  520.9 6.0 multiply_reduce_fusion
  586.9 5.1 convert_reduce_fusion.4
  647.4 6.2 pad_maximum_fusion.2
  654.4 6.7 multiply_convert_fusion
  662.8 5.5 fusion.102
  674.0 5.6 fusion.88
  679.6 332.9 %fusion.90 = (f32[8,768]{1,0:T(8,128)S(1)}, f32[8,768]{1,0:T(8,128)S(1)}, f32[8,3072]{1,0:T(8,128)S(1)}) fusion(f32[768,768]{1,0:T(8,128)} %fusion.80, f32[768,768]{1,0:T(8,128)S(1)} %copy-done.16, f32[768,3072]{1,0:T(8,128)} %fusion.88), kind=kCustom, calls=%all-reduce-scatter.3 | all-reduce-scatter fusion | flops 4718593 | bytes 14303232
  1022.9 5.0 collective-permute-done.31
  1029.8 27.1 %collective-permute-done.32 = f32[8,768]{1,0:T(8,128)S(1)} collective-permute-done((f32[8,768]{1,0:T(8,128)S(1)}, f32[8,768]{1,0:T(8,128)S(1)}, u32[]{:S(2)}, u32[]{:S(2)}) %collective-permute-start.32) | collective-permute-done | bytes 24608
  1059.5 6.8 collective-permute-start.38
  1066.3 11.9 collective-permute-start.39
  1157.4 7.3 add_convert_fusion
  1210.5 82.1 %all-reduce.16 = (f32[3,768]{1,0:T(4,128)S(1)}, f32[3,768]{1,0:T(4,128)S(1)}, f32[3,768]{1,0:T(4,128)S(1)}, f32[3,768]{1,0:T(4,128)S(1)}, f32[3072]{0:T(1024)S(1)}, /*index=5*/f32[768]{0:T(1024)S(1)}) all-reduce(f32[3,768]{1,0:T(4,128)S(1)} %pad_maximum_fusion.3, ...), channel_id=2, replica_groups=mesh['dp'=16,'fsdp'=8] {'dp','fsdp'}, use_global_device_ids=true, to_apply=%region_21.22.clone | all-reduce | flops 13056 | bytes 104448
  1298.9 5.0 collective-permute-start.67
  1348.2 4.9 concatenate.1
  1353.2 16.8 %concatenate = f32[262,768]{1,0:T(8,128)S(1)} concatenate(f32[6,768]{1,0:T(8,128)S(1)} %collective-permute-done.31, f32[8,768]{1,0:T(8,128)} %copy-done.160, f32[8,768]{1,0:T(8,128)} %copy-done.158, f32[8,768]{1,0:T(8,128)} %copy-done.157, f32[8,768]{1,0:T(8,128)} %copy-done.156, f32[8,768]{1,0:T(8,128)} %copy-done.155, f32[8,768]{1,0:T(8,128)} %copy-done.154, ...), dimensions={0} | concatenate | bytes 1609728
  1394.9 5.2 collective-permute-done.91
  1405.9 31.5 %concatenate.2 = f32[262,3072]{1,0:T(8,128)S(1)} concatenate(f32[6,3072]{1,0:T(8,128)S(1)} %collective-permute-done.95, f32[8,3072]{1,0:T(8,128)} %collective-permute-done.94, f32[8,3072]{1,0:T(8,128)} %copy-done.77, f32[8,3072]{1,0:T(8,128)} %copy-done.76, f32[8,3072]{1,0:T(8,128)} %copy-done.75, f32[8,3072]{1,0:T(8,128)} %copy-done.74, f32[8,3072]{1,0:T(8,128)} %copy-done.73, ...), dimensions={0} | concatenate | bytes 6438912
  (768 shorter events, 450.3 us)
Async XLA Ops:
  7.2 214.7 %all-gather.23.cloned.1.call-start = ((), (), s32[]{:S(2)}) async-start(), calls=%async_computation.8 | async-start | bytes 1585152 | tf_op jit(solution)/shard_map/all_gather | solution.py:168
  8.0 217.2 %all-gather.25.cloned.1.call-start = ((), (), s32[]{:S(2)}) async-start(), calls=%async_computation.9 | async-start | bytes 1585152 | tf_op jit(solution)/shard_map/all_gather | solution.py:171
  8.7 219.6 %all-gather.15.cloned.1.call-start = ((), (), s32[]{:S(2)}) async-start(), calls=%async_computation.2 | async-start | bytes 3170304 | tf_op jit(solution)/shard_map/all_gather | solution.py:177
  9.5 265.0 %all-gather.17.cloned.1.call-start = ((), (), s32[]{:S(2)}) async-start(), calls=%async_computation.3 | async-start | bytes 4755456 | tf_op jit(solution)/shard_map/all_gather | solution.py:167
  10.9 331.6 %all-gather.19.cloned.1.call-start = ((), (), s32[]{:S(2)}) async-start(), calls=%async_computation.4 | async-start | bytes 4755456 | tf_op jit(solution)/shard_map/all_gather | solution.py:170
  12.4 397.6 %all-gather.21.cloned.1.call-start = ((), (), s32[]{:S(2)}) async-start(), calls=%async_computation.5 | async-start | bytes 4755456 | tf_op jit(solution)/shard_map/all_gather | solution.py:175
  13.0 466.0 %all-gather.27.cloned.1.call-start = ((), (), s32[]{:S(2)}) async-start(), calls=%async_computation.10 | async-start | bytes 6340608 | tf_op jit(solution)/shard_map/all_gather | solution.py:173
  13.7 1424.3 %all-reduce.22.cloned.1.call-start = ((), (), s32[]{:S(2)}) async-start(), calls=%async_computation.11 | async-start | bytes 28311552
  628.9 812.2 %reduce-scatter.17.cloned.1.call-start = ((), (), s32[]{:S(2)}) async-start(), calls=%async_computation.7 | async-start | bytes 6340608 | tf_op jit(solution)/shard_map/reduce_scatter | solution.py:307
  653.7 787.5 %reduce-scatter.15.cloned.1.call-start = ((), (), s32[]{:S(2)}) async-start(), calls=%async_computation.6 | async-start | bytes 9510912 | tf_op jit(solution)/shard_map/reduce_scatter | solution.py:305
  1013.8 43.1 %collective-permute-start.32 = (f32[8,768]{1,0:T(8,128)S(1)}, f32[8,768]{1,0:T(8,128)S(1)}, u32[]{:S(2)}, u32[]{:S(2)}) collective-permute-start(f32[8,768]{1,0:T(8,128)S(1)} %get-tuple-element.53), channel_id=1, source_target_pairs={{0,1},{1,2},{2,3},{3,4},{4,5},{5,6},{6,7},{7,8},{8,9},{9,10},{10,1... | collective-permute-start | bytes 73736
  1015.8 43.8 %collective-permute-start.33 = (f32[8,768]{1,0:T(8,128)S(1)}, f32[8,768]{1,0:T(8,128)S(1)}, u32[]{:S(2)}, u32[]{:S(2)}) collective-permute-start(f32[8,768]{1,0:T(8,128)S(1)} %get-tuple-element.53), channel_id=1, source_target_pairs={{0,2},{1,3},{2,4},{3,5},{4,6},{5,7},{6,8},{7,9},{8,10},{9,11},{10,... | collective-permute-start | bytes 73736
  1017.7 48.6 %collective-permute-start.34 = (f32[8,768]{1,0:T(8,128)S(1)}, f32[8,768]{1,0:T(8,128)S(1)}, u32[]{:S(2)}, u32[]{:S(2)}) collective-permute-start(f32[8,768]{1,0:T(8,128)S(1)} %get-tuple-element.53), channel_id=1, source_target_pairs={{0,3},{1,4},{2,5},{3,6},{4,7},{5,8},{6,9},{7,10},{8,11},{9,12},{10... | collective-permute-start | bytes 73736
  1019.6 58.6 %collective-permute-start.35 = (f32[8,768]{1,0:T(8,128)S(1)}, f32[8,768]{1,0:T(8,128)S(1)}, u32[]{:S(2)}, u32[]{:S(2)}) collective-permute-start(f32[8,768]{1,0:T(8,128)S(1)} %get-tuple-element.53), channel_id=1, source_target_pairs={{0,4},{1,5},{2,6},{3,7},{4,8},{5,9},{6,10},{7,11},{8,12},{9,13},{1... | collective-permute-start | bytes 73736
  1027.9 52.3 %collective-permute-start.36 = (f32[8,768]{1,0:T(8,128)S(1)}, f32[8,768]{1,0:T(8,128)S(1)}, u32[]{:S(2)}, u32[]{:S(2)}) collective-permute-start(f32[8,768]{1,0:T(8,128)S(1)} %get-tuple-element.53), channel_id=1, source_target_pairs={{0,5},{1,6},{2,7},{3,8},{4,9},{5,10},{6,11},{7,12},{8,13},{9,14},{... | collective-permute-start | bytes 73736
  1056.9 26.4 %collective-permute-start.37 = (f32[8,768]{1,0:T(8,128)S(1)}, f32[8,768]{1,0:T(8,128)S(1)}, u32[]{:S(2)}, u32[]{:S(2)}) collective-permute-start(f32[8,768]{1,0:T(8,128)S(1)} %get-tuple-element.53), channel_id=1, source_target_pairs={{0,6},{1,7},{2,8},{3,9},{4,10},{5,11},{6,12},{7,13},{8,14},{9,15},... | collective-permute-start | bytes 73736
  1059.5 25.7 %collective-permute-start.38 = (f32[8,768]{1,0:T(8,128)S(1)}, f32[8,768]{1,0:T(8,128)S(1)}, u32[]{:S(2)}, u32[]{:S(2)}) collective-permute-start(f32[8,768]{1,0:T(8,128)S(1)} %get-tuple-element.53), channel_id=1, source_target_pairs={{0,7},{1,8},{2,9},{3,10},{4,11},{5,12},{6,13},{7,14},{8,15},{9,16}... | collective-permute-start | bytes 73736
  1066.3 20.9 %collective-permute-start.39 = (f32[8,768]{1,0:T(8,128)S(1)}, f32[8,768]{1,0:T(8,128)S(1)}, u32[]{:S(2)}, u32[]{:S(2)}) collective-permute-start(f32[8,768]{1,0:T(8,128)S(1)} %get-tuple-element.53), channel_id=1, source_target_pairs={{0,8},{1,9},{2,10},{3,11},{4,12},{5,13},{6,14},{7,15},{8,16},{9,17... | collective-permute-start | bytes 73736
  1147.0 18.0 %collective-permute-start.16 = (f32[8,768]{1,0:T(8,128)S(1)}, f32[8,768]{1,0:T(8,128)S(1)}, u32[]{:S(2)}, u32[]{:S(2)}) collective-permute-start(f32[8,768]{1,0:T(8,128)S(1)} %get-tuple-element.52), channel_id=1, source_target_pairs={{0,17},{1,18},{2,19},{3,20},{4,21},{5,22},{6,23},{7,24},{8,25},{9,... | collective-permute-start | bytes 73736
  1149.0 17.9 %collective-permute-start.17 = (f32[8,768]{1,0:T(8,128)S(1)}, f32[8,768]{1,0:T(8,128)S(1)}, u32[]{:S(2)}, u32[]{:S(2)}) collective-permute-start(f32[8,768]{1,0:T(8,128)S(1)} %get-tuple-element.52), channel_id=1, source_target_pairs={{0,18},{1,19},{2,20},{3,21},{4,22},{5,23},{6,24},{7,25},{8,26},{9,... | collective-permute-start | bytes 73736
  1151.0 17.9 %collective-permute-start.18 = (f32[8,768]{1,0:T(8,128)S(1)}, f32[8,768]{1,0:T(8,128)S(1)}, u32[]{:S(2)}, u32[]{:S(2)}) collective-permute-start(f32[8,768]{1,0:T(8,128)S(1)} %get-tuple-element.52), channel_id=1, source_target_pairs={{0,19},{1,20},{2,21},{3,22},{4,23},{5,24},{6,25},{7,26},{8,27},{9,... | collective-permute-start | bytes 73736
  1200.9 106.7 %collective-permute-start.64 = (f32[8,3072]{1,0:T(8,128)S(1)}, f32[8,3072]{1,0:T(8,128)S(1)}, u32[]{:S(2)}, u32[]{:S(2)}) collective-permute-start(f32[8,3072]{1,0:T(8,128)S(1)} %get-tuple-element.54), channel_id=1, source_target_pairs={{0,1},{1,2},{2,3},{3,4},{4,5},{5,6},{6,7},{7,8},{8,9},{9,10},{10,1... | collective-permute-start | bytes 294920
  1203.0 90.8 %collective-permute-start.7 = (f32[8,768]{1,0:T(8,128)S(1)}, f32[8,768]{1,0:T(8,128)S(1)}, u32[]{:S(2)}, u32[]{:S(2)}) collective-permute-start(f32[8,768]{1,0:T(8,128)S(1)} %get-tuple-element.52), channel_id=1, source_target_pairs={{0,8},{1,9},{2,10},{3,11},{4,12},{5,13},{6,14},{7,15},{8,16},{9,17... | collective-permute-start | bytes 73736
  1204.9 92.0 %collective-permute-start.8 = (f32[8,768]{1,0:T(8,128)S(1)}, f32[8,768]{1,0:T(8,128)S(1)}, u32[]{:S(2)}, u32[]{:S(2)}) collective-permute-start(f32[8,768]{1,0:T(8,128)S(1)} %get-tuple-element.52), channel_id=1, source_target_pairs={{0,9},{1,10},{2,11},{3,12},{4,13},{5,14},{6,15},{7,16},{8,17},{9,1... | collective-permute-start | bytes 73736
  1206.9 92.0 %collective-permute-start.9 = (f32[8,768]{1,0:T(8,128)S(1)}, f32[8,768]{1,0:T(8,128)S(1)}, u32[]{:S(2)}, u32[]{:S(2)}) collective-permute-start(f32[8,768]{1,0:T(8,128)S(1)} %get-tuple-element.52), channel_id=1, source_target_pairs={{0,10},{1,11},{2,12},{3,13},{4,14},{5,15},{6,16},{7,17},{8,18},{9,... | collective-permute-start | bytes 73736
  1209.2 94.8 %collective-permute-start.95 = (f32[6,3072]{1,0:T(8,128)S(1)}, f32[6,3072]{1,0:T(8,128)S(1)}, u32[]{:S(2)}, u32[]{:S(2)}) collective-permute-start(f32[6,3072]{1,0:T(8,128)S(1)} %slice.111), channel_id=1, source_target_pairs={{0,32},{1,33},{2,34},{3,35},{4,36},{5,37},{6,38},{7,39},{8,40},{9,... | collective-permute-start | bytes 221192
  1298.9 18.3 %collective-permute-start.67 = (f32[8,3072]{1,0:T(8,128)S(1)}, f32[8,3072]{1,0:T(8,128)S(1)}, u32[]{:S(2)}, u32[]{:S(2)}) collective-permute-start(f32[8,3072]{1,0:T(8,128)S(1)} %get-tuple-element.54), channel_id=1, source_target_pairs={{0,4},{1,5},{2,6},{3,7},{4,8},{5,9},{6,10},{7,11},{8,12},{9,13},{1... | collective-permute-start | bytes 294920
  1336.7 33.2 %collective-permute-start.80 = (f32[8,3072]{1,0:T(8,128)S(1)}, f32[8,3072]{1,0:T(8,128)S(1)}, u32[]{:S(2)}, u32[]{:S(2)}) collective-permute-start(f32[8,3072]{1,0:T(8,128)S(1)} %get-tuple-element.54), channel_id=1, source_target_pairs={{0,17},{1,18},{2,19},{3,20},{4,21},{5,22},{6,23},{7,24},{8,25},{9,... | collective-permute-start | bytes 294920
  1338.7 33.3 %collective-permute-start.81 = (f32[8,3072]{1,0:T(8,128)S(1)}, f32[8,3072]{1,0:T(8,128)S(1)}, u32[]{:S(2)}, u32[]{:S(2)}) collective-permute-start(f32[8,3072]{1,0:T(8,128)S(1)} %get-tuple-element.54), channel_id=1, source_target_pairs={{0,18},{1,19},{2,20},{3,21},{4,22},{5,23},{6,24},{7,25},{8,26},{9,... | collective-permute-start | bytes 294920
  1340.7 33.2 %collective-permute-start.82 = (f32[8,3072]{1,0:T(8,128)S(1)}, f32[8,3072]{1,0:T(8,128)S(1)}, u32[]{:S(2)}, u32[]{:S(2)}) collective-permute-start(f32[8,3072]{1,0:T(8,128)S(1)} %get-tuple-element.54), channel_id=1, source_target_pairs={{0,19},{1,20},{2,21},{3,22},{4,23},{5,24},{6,25},{7,26},{8,27},{9,... | collective-permute-start | bytes 294920
  1343.3 32.5 %collective-permute-start.83 = (f32[8,3072]{1,0:T(8,128)S(1)}, f32[8,3072]{1,0:T(8,128)S(1)}, u32[]{:S(2)}, u32[]{:S(2)}) collective-permute-start(f32[8,3072]{1,0:T(8,128)S(1)} %get-tuple-element.54), channel_id=1, source_target_pairs={{0,20},{1,21},{2,22},{3,23},{4,24},{5,25},{6,26},{7,27},{8,28},{9,... | collective-permute-start | bytes 294920
  1345.3 32.5 %collective-permute-start.84 = (f32[8,3072]{1,0:T(8,128)S(1)}, f32[8,3072]{1,0:T(8,128)S(1)}, u32[]{:S(2)}, u32[]{:S(2)}) collective-permute-start(f32[8,3072]{1,0:T(8,128)S(1)} %get-tuple-element.54), channel_id=1, source_target_pairs={{0,21},{1,22},{2,23},{3,24},{4,25},{5,26},{6,27},{7,28},{8,29},{9,... | collective-permute-start | bytes 294920
  (274 other events, 12644.9 us)
Sparse Core Ops, SparseCore 0:
  10.9 64.4 all-gather.22
  78.2 61.5 all-gather.24
  142.7 63.6 all-gather.14
  209.9 64.5 all-gather.16
  277.9 64.5 all-gather.18
  345.4 64.5 all-gather.20
  413.1 65.8 all-gather.26
  629.0 176.5 all-reduce.21
  811.8 214.5 reduce-scatter.16
  1031.9 216.4 reduce-scatter.14
where the time goes:
time: 1470 us; the launch traced here: 1450 us
  blocking collectives  615 us (42%)
  starting transfers between devices  211 us (14%)
  local copies, waits for them, and re-layouts  202 us (14%)
  waiting for transfers between devices  189 us (13%)
  matrix products  153 us (10%)
  other arithmetic  59.2 us (4%)
  between operations  20.1 us (1%)
    unnamed x3, blocking collectives  479 us
    unnamed x97, starting transfers between devices  211 us
    unnamed x428, local copies, waits for them, and re-layouts  93.9 us
    unnamed x107, waiting for transfers between devices  64.5 us
    all_gather x1, waiting for transfers between devices, on_device(): lax.all_gather(ffn_up, ('dp', 'fsdp'), axis=0, tiled=True)  62.1 us
    dot_general x10, matrix products, product(): return jnp.dot(left_arr, right_arr, preferred_element_type=jnp.float32)  47.3 us
    all_gather x1, waiting for transfers between devices, on_device(): lax.all_gather(row_qkv, ('dp', 'fsdp'), axis=1, tiled=True)  41.3 us
    all_gather x1, blocking collectives, on_device(): lax.all_gather(norm_gain, ('dp', 'fsdp'), axis=1, tiled=True)  36.8 us
  transfers between devices with their start and end apart: 106, of which 37 were waited for; matrix products, arithmetic and copies ran while one was open for 40% of the time, Pallas kernels for 0%

commit v1 on v0

--- a/solution.py
+++ b/solution.py
@@ -3,7 +3,7 @@
 import jax
 import jax.numpy as jnp
 from jax import lax
-from jax.sharding import PartitionSpec as P
+from jax.sharding import Mesh, PartitionSpec as P
 
 HEADS = 12
 HEAD_DIM = 64
@@ -13,6 +13,84 @@
 eps = 1e-05
 row_forms = ("rihe,rjhe->hij", "hij,rjhe->rihe", "hij,rihe->rjhe")
 col_forms = ("rche,tche->chrt", "chrt,tche->rche", "chrt,rche->tche")
+
+AXES = ("y", "z", "x", "c")
+
+DEVICES = 128
+LANES = 128
+
+
+def gather_weights(*pieces):
+    flat = jnp.concatenate([piece.reshape(-1) for piece, _ in pieces])
+    count = flat.shape[0]
+    padded = -(-count // (8 * LANES)) * 8 * LANES
+    flat = jnp.pad(flat, (0, padded - count)).reshape(-1, LANES)
+    whole = lax.all_gather(flat, AXES, axis=0, tiled=False).reshape(DEVICES, padded)
+    outs, start = [], 0
+    for piece, dim in pieces:
+        part = whole[:, start : start + piece.size].reshape((DEVICES,) + piece.shape)
+        start += piece.size
+        part = jnp.moveaxis(part, 0, dim)
+        outs.append(
+            part.reshape(piece.shape[:dim] + (DEVICES * piece.shape[dim],) + piece.shape[dim + 1 :])
+        )
+    return outs
+
+
+def take(value, index, dim):
+    return lax.squeeze(lax.dynamic_slice_in_dim(value, index, 1, dim), (dim,))
+
+
+def shift(value, axis, forward):
+    pairs = []
+    for place in range(4):
+        for core in range(2):
+            step = 1 if (core == 0) == forward else -1
+            pairs.append((place * 2 + core, ((place + step) % 4) * 2 + core))
+    return lax.ppermute(value, (axis, "c"), pairs)
+
+
+def ring_scatter(value, axis, dim):
+    place, step = lax.axis_index(axis), 1 - 2 * lax.axis_index("c")
+    far = shift(take(value, (place + 2) % 4, dim), axis, True)
+    behind = shift(take(value, (place - step) % 4, dim), axis, False)
+    ahead = take(value, (place + step) % 4, dim).astype(jnp.float32) + far.astype(jnp.float32)
+    ahead = shift(ahead.astype(jnp.bfloat16), axis, True)
+    own = take(value, place, dim).astype(jnp.float32)
+    return (own + behind.astype(jnp.float32) + ahead.astype(jnp.float32)).astype(jnp.bfloat16)
+
+
+def reduce_packed(packed):
+    core = lax.axis_index("c")
+    swapped = lax.ppermute(take(packed, 1 - core, 3), "c", [(0, 1), (1, 0)])
+    both = take(packed, core, 3).astype(jnp.float32) + swapped.astype(jnp.float32)
+    both = both.astype(jnp.bfloat16)
+    third = both.shape[3] // 3
+    one, two, three = (both[..., i * third : (i + 1) * third, :] for i in range(3))
+    one, two, three = ring_scatter(one, "x", 2), ring_scatter(two, "y", 0), ring_scatter(three, "z", 1)
+    one, two, three = ring_scatter(one, "y", 0), ring_scatter(two, "z", 0), ring_scatter(three, "x", 1)
+    one, two, three = ring_scatter(one, "z", 0), ring_scatter(two, "x", 0), ring_scatter(three, "y", 0)
+    return jnp.concatenate([one, two, three], 0)
+
+
+def scatter_grads(*pieces):
+    parts = []
+    for piece, dim in pieces:
+        shape = piece.shape
+        split = piece.reshape(shape[:dim] + (DEVICES, shape[dim] // DEVICES) + shape[dim + 1 :])
+        parts.append(jnp.moveaxis(split, dim, 0).reshape(DEVICES, -1).astype(jnp.bfloat16))
+    flat = jnp.concatenate(parts, 1)
+    count = flat.shape[1]
+    padded = -(-count // (24 * LANES)) * 24 * LANES
+    flat = jnp.pad(flat, ((0, 0), (0, padded - count))).reshape(4, 4, 4, 2, -1, LANES)
+    mine = reduce_packed(flat).reshape(-1)
+    outs, start = [], 0
+    for piece, dim in pieces:
+        shape = piece.shape[:dim] + (piece.shape[dim] // DEVICES,) + piece.shape[dim + 1 :]
+        size = math.prod(shape)
+        outs.append(mine[start : start + size].reshape(shape).astype(jnp.float32))
+        start += size
+    return outs
 
 
 def product(left_arr, right_arr):
@@ -161,20 +239,20 @@
         down_weight,
         down_biases,
         tables,
-    ) = (
-        lax.all_gather(norm_gain, ("dp", "fsdp"), axis=1, tiled=True),
-        lax.all_gather(norm_bias, ("dp", "fsdp"), axis=1, tiled=True),
-        lax.all_gather(row_qkv, ("dp", "fsdp"), axis=1, tiled=True),
-        lax.all_gather(row_out, ("dp", "fsdp"), axis=0, tiled=True),
-        lax.all_gather(row_bias, ("dp", "fsdp"), axis=1, tiled=True),
-        lax.all_gather(col_qkv, ("dp", "fsdp"), axis=1, tiled=True),
-        lax.all_gather(col_out, ("dp", "fsdp"), axis=0, tiled=True),
-        lax.all_gather(col_bias, ("dp", "fsdp"), axis=1, tiled=True),
-        lax.all_gather(ffn_up, ("dp", "fsdp"), axis=0, tiled=True),
-        lax.all_gather(up_bias, ("dp", "fsdp"), axis=0, tiled=True),
-        lax.all_gather(ffn_down, ("dp", "fsdp"), axis=0, tiled=True),
-        lax.all_gather(down_bias, ("dp", "fsdp"), axis=0, tiled=True),
-        lax.all_gather(pos_tables, ("dp", "fsdp"), axis=1, tiled=True),
+    ) = gather_weights(
+        (norm_gain, 1),
+        (norm_bias, 1),
+        (row_qkv, 1),
+        (row_out, 0),
+        (row_bias, 1),
+        (col_qkv, 1),
+        (col_out, 0),
+        (col_bias, 1),
+        (ffn_up, 0),
+        (up_bias, 0),
+        (ffn_down, 0),
+        (down_bias, 0),
+        (pos_tables, 1),
     )
     gain_rows = norm_gains.astype(jnp.float32)
     shift_rows = norm_shifts.astype(jnp.float32)
@@ -205,36 +283,6 @@
     act_low = act_value.astype(jnp.bfloat16)
     hidden_out = hidden_late + product(act_low, down_weight) + down_biases
     activations = hidden_out.reshape(tokens.shape).astype(jnp.bfloat16)
-    (
-        norm_gains,
-        norm_shifts,
-        row_proj,
-        row_output,
-        row_biases,
-        col_proj,
-        col_output,
-        col_biases,
-        up_weight,
-        up_biases,
-        down_weight,
-        down_biases,
-        tables,
-    ) = (
-        lax.all_gather(norm_gain, ("dp", "fsdp"), axis=1, tiled=True),
-        lax.all_gather(norm_bias, ("dp", "fsdp"), axis=1, tiled=True),
-        lax.all_gather(row_qkv, ("dp", "fsdp"), axis=1, tiled=True),
-        lax.all_gather(row_out, ("dp", "fsdp"), axis=0, tiled=True),
-        lax.all_gather(row_bias, ("dp", "fsdp"), axis=1, tiled=True),
-        lax.all_gather(col_qkv, ("dp", "fsdp"), axis=1, tiled=True),
-        lax.all_gather(col_out, ("dp", "fsdp"), axis=0, tiled=True),
-        lax.all_gather(col_bias, ("dp", "fsdp"), axis=1, tiled=True),
-        lax.all_gather(ffn_up, ("dp", "fsdp"), axis=0, tiled=True),
-        lax.all_gather(up_bias, ("dp", "fsdp"), axis=0, tiled=True),
-        lax.all_gather(ffn_down, ("dp", "fsdp"), axis=0, tiled=True),
-        lax.all_gather(down_bias, ("dp", "fsdp"), axis=0, tiled=True),
-        lax.all_gather(pos_tables, ("dp", "fsdp"), axis=1, tiled=True),
-    )
-    gain_rows = norm_gains.astype(jnp.float32)
     grad_out = (cotangent[0].astype(jnp.float32) * valid_cols[None, :, None]).reshape(
         token_count, model_width
     )
@@ -291,20 +339,20 @@
         down_grad,
         down_bias_grad,
         table_grad,
-    ) = (
-        lax.psum_scatter(gain_grad, ("dp", "fsdp"), scatter_dimension=1, tiled=True),
-        lax.psum_scatter(shift_grad, ("dp", "fsdp"), scatter_dimension=1, tiled=True),
-        lax.psum_scatter(row_proj_grad, ("dp", "fsdp"), scatter_dimension=1, tiled=True),
-        lax.psum_scatter(row_output_grad, ("dp", "fsdp"), scatter_dimension=0, tiled=True),
-        lax.psum_scatter(row_bias_grad, ("dp", "fsdp"), scatter_dimension=1, tiled=True),
-        lax.psum_scatter(col_proj_grad, ("dp", "fsdp"), scatter_dimension=1, tiled=True),
-        lax.psum_scatter(col_output_grad, ("dp", "fsdp"), scatter_dimension=0, tiled=True),
-        lax.psum_scatter(col_bias_grad, ("dp", "fsdp"), scatter_dimension=1, tiled=True),
-        lax.psum_scatter(up_grad, ("dp", "fsdp"), scatter_dimension=0, tiled=True),
-        lax.psum_scatter(up_bias_grad, ("dp", "fsdp"), scatter_dimension=0, tiled=True),
-        lax.psum_scatter(down_grad, ("dp", "fsdp"), scatter_dimension=0, tiled=True),
-        lax.psum_scatter(down_bias_grad, ("dp", "fsdp"), scatter_dimension=0, tiled=True),
-        lax.psum_scatter(table_grad, ("dp", "fsdp"), scatter_dimension=1, tiled=True),
+    ) = scatter_grads(
+        (gain_grad, 1),
+        (shift_grad, 1),
+        (row_proj_grad, 1),
+        (row_output_grad, 0),
+        (row_bias_grad, 1),
+        (col_proj_grad, 1),
+        (col_output_grad, 0),
+        (col_bias_grad, 1),
+        (up_grad, 0),
+        (up_bias_grad, 0),
+        (down_grad, 0),
+        (down_bias_grad, 0),
+        (table_grad, 1),
     )
     tokens_grad = grad_input.reshape(tokens.shape)
     return (
@@ -327,42 +375,43 @@
 
 
 def solution(mesh):
+    mesh = Mesh(mesh.devices.reshape(4, 4, 4, 2), AXES)
     in_specs = (
-        P(("dp", "fsdp"), None, None, None),
-        P(("dp", "fsdp"), None, None, None),
-        P(("dp", "fsdp")),
-        P(("dp", "fsdp")),
-        P(("dp", "fsdp")),
-        P(None, ("dp", "fsdp")),
-        P(None, ("dp", "fsdp")),
-        P(None, ("dp", "fsdp"), None),
-        P(("dp", "fsdp"), None),
-        P(None, ("dp", "fsdp")),
-        P(None, ("dp", "fsdp"), None),
-        P(("dp", "fsdp"), None),
-        P(None, ("dp", "fsdp")),
-        P(("dp", "fsdp"), None),
-        P(("dp", "fsdp")),
-        P(("dp", "fsdp"), None),
-        P(("dp", "fsdp")),
-        P(None, ("dp", "fsdp"), None),
+        P(AXES, None, None, None),
+        P(AXES, None, None, None),
+        P(AXES),
+        P(AXES),
+        P(AXES),
+        P(None, AXES),
+        P(None, AXES),
+        P(None, AXES, None),
+        P(AXES, None),
+        P(None, AXES),
+        P(None, AXES, None),
+        P(AXES, None),
+        P(None, AXES),
+        P(AXES, None),
+        P(AXES),
+        P(AXES, None),
+        P(AXES),
+        P(None, AXES, None),
     )
     out_specs = (
-        P(("dp", "fsdp"), None, None, None),
-        P(("dp", "fsdp"), None, None, None),
-        P(None, ("dp", "fsdp")),
-        P(None, ("dp", "fsdp")),
-        P(None, ("dp", "fsdp"), None),
-        P(("dp", "fsdp"), None),
-        P(None, ("dp", "fsdp")),
-        P(None, ("dp", "fsdp"), None),
-        P(("dp", "fsdp"), None),
-        P(None, ("dp", "fsdp")),
-        P(("dp", "fsdp"), None),
-        P(("dp", "fsdp")),
-        P(("dp", "fsdp"), None),
-        P(("dp", "fsdp")),
-        P(None, ("dp", "fsdp"), None),
+        P(AXES, None, None, None),
+        P(AXES, None, None, None),
+        P(None, AXES),
+        P(None, AXES),
+        P(None, AXES, None),
+        P(AXES, None),
+        P(None, AXES),
+        P(None, AXES, None),
+        P(AXES, None),
+        P(None, AXES),
+        P(AXES, None),
+        P(AXES),
+        P(AXES, None),
+        P(AXES),
+        P(None, AXES, None),
     )
     return jax.shard_map(
         on_device, mesh=mesh, in_specs=in_specs, out_specs=out_specs, check_vma=False

time: 1470 us -> 963 us (0.66)
  blocking collectives: 615 us -> 0 us
  local copies, waits for them, and re-layouts: 202 us -> 534 us
  starting transfers between devices: 211 us -> 31.5 us
  waiting for transfers between devices: 189 us -> 132 us
  other arithmetic: 59.2 us -> 76.4 us
    unnamed x3 -> x0, blocking collectives: 479 us -> none
    unnamed x97 -> x0, starting transfers between devices: 211 us -> none
    all_gather x4 -> x0, blocking collectives: 136 us -> none  [the longest x1 36.8 us: on_device(): lax.all_gather(norm_gain, ('dp', 'fsdp'), axis=1, tiled=True)]
    unnamed x428 -> x138, local copies, waits for them, and re-layouts: 93.9 us -> 192 us
    unnamed x107 -> x1, waiting for transfers between devices: 64.5 us -> 0.02 us
    convert_element_type x0 -> x43, local copies, waits for them, and re-layouts: none -> 63.8 us  [the longest x20 57.4 us: scatter_grads(): jnp.moveaxis(split, dim, 0).reshape(DEVICES, -1).astype(jnp.bfloat16)]
    slice x0 -> x17, local copies, waits for them, and re-layouts: none -> 60.9 us  [the longest x8 38.3 us: gather_weights(): part = whole[:, start:start + piece.size].reshape((DEVICES,) + piece.shape)]
    ppermute x0 -> x28, waiting for transfers between devices: none -> 46.2 us  [the longest x27 28.7 us: shift(): return lax.ppermute(value, (axis, 'c'), pairs)]
  transfers between devices with their start and end apart: 106 -> 29, of which waited for: 37 -> 12; matrix products, arithmetic and copies ran while one was open for 40% -> 3% of each run, Pallas kernels for 0% -> 0%
where the time goes in v1:
time: 963 us; the launch traced here: 944 us
  local copies, waits for them, and re-layouts  534 us (55%)
  matrix products  152 us (16%)
  waiting for transfers between devices  132 us (14%)
  other arithmetic  76.4 us (8%)
  starting transfers between devices  31.5 us (3%)
  between operations  17.8 us (2%)
    unnamed x138, local copies, waits for them, and re-layouts  192 us
    all_gather x1, waiting for transfers between devices, gather_weights(): lax.all_gather(flat, AXES, axis=0, tiled=False).reshape(DEVICES, padded)  86.1 us
    convert_element_type x20, local copies, waits for them, and re-layouts, scatter_grads(): jnp.moveaxis(split, dim, 0).reshape(DEVICES, -1).astype(jnp.bfloat16)  57.4 us
    dot_general x10, matrix products, product(): return jnp.dot(left_arr, right_arr, preferred_element_type=jnp.float32)  49 us
    slice x8, local copies, waits for them, and re-layouts, gather_weights(): part = whole[:, start:start + piece.size].reshape((DEVICES,) + piece.shape)  38.3 us
    all_gather x1, local copies, waits for them, and re-layouts, gather_weights(): lax.all_gather(flat, AXES, axis=0, tiled=False).reshape(DEVICES, padded)  31.3 us
    dot_general x10, matrix products, product_nt(): lax.dot_general(left_arr, right_arr, (((1,), (1,)), ((), ())), preferred_...  31.2 us
    ppermute x27, starting transfers between devices, shift(): return lax.ppermute(value, (axis, 'c'), pairs)  31.1 us
  transfers between devices with their start and end apart: 29, of which 12 were waited for; matrix products, arithmetic and copies ran while one was open for 3% of the time, Pallas kernels for 0%

profile of v1, /device:TPU:24, one launch (start us, length us, event | category | flops | bytes accessed | tf_op | source)
XLA Modules:
  0.0 944.3 jit_solution(5623667994262857853)
XLA Ops:
  25.4 86.1 %all-gather.2.cloned.1.call-done = bf16[128,680,128]{2,1,0:T(8,128)(2,1)} async-done(((bf16[1,680,128]{2,1,0:T(8,128)(2,1)}), bf16[128,680,128]{2,1,0:T(8,128)(2,1)}) %all-gather.2.cloned.1.call-update) | async-done | bytes 22282256 | tf_op jit(solution)/shard_map/all_gather | solution.py:28
  111.6 31.3 %copy.249 = bf16[128,680,128]{0,2,1:T(8,128)(2,1)} copy(bf16[128,680,128]{2,1,0:T(8,128)(2,1)} %all-gather.2.cloned.1.call-done) | data formatting | bytes 44564480 | tf_op jit(solution)/shard_map/all_gather | solution.py:28
  161.1 5.8 fusion.128
  166.9 8.2 fusion.125
  243.4 6.7 copy.288
  250.1 9.5 %reshape_reshape.18 = bf16[768,3072]{1,0:T(8,128)(2,1)} reshape(bf16[128,18432]{1,0:T(8,128)(2,1)} %copy.288) | data formatting | bytes 9437184 | tf_op jit(solution)/shard_map/reshape;reshape | solution.py:35
  306.6 22.4 %fusion.137 = (f32[64,12,8]{2,1,0:T(8,128)S(1)}, f32[64,12,8,8]{2,3,1,0:T(8,128)S(1)}) fusion(f32[64,12,8,8]{2,3,1,0:T(8,128)S(1)} %fusion.63), kind=kOutput, calls=%fused_computation.300 | output fusion | flops 196615 | bytes 417792 | tf_op jit(solution)/shard_map/sub | solution.py:149
  344.1 6.9 copy.290
  350.9 7.8 reshape_reshape.19
  358.7 5.4 convolution_convert_fusion.2
  364.1 21.1 %fusion.122 = (bf16[3072]{0:T(1024)(128)(2,1)S(1)}, bf16[512,3072]{1,0:T(8,128)(2,1)S(1)}, f32[512,3072]{1,0:T(8,128)}, f32[512,3072]{1,0:T(8,128)}) fusion(bf16[512,3072]{1,0:T(8,128)(2,1)S(1)} %convolution_convert_fusion.2, f32[3072]{0:T(1024)S(1)} %reshape.981, bf16[768,3072]{1,0:T(8,128)(2,1)} %reshape_reshape.18, f32[512,768]{1,0:T(8,128)S(1)} %copy-done.16, ...), kind=kOutput, calls=%fused_computation.287 | convolution fusion | flops 2535846912 | bytes 25194496 | tf_op jit(solution)/shard_map/dot_general | solution.py:97
  399.9 5.9 multiply_reduce_fusion
  512.8 9.4 convert_element_type.838
  526.8 6.0 copy.338
  532.8 5.9 copy.347
  569.9 6.1 copy.345
  576.0 6.2 multiply_convert_fusion
  588.2 7.7 convert_element_type.842
  599.0 22.4 %dynamic-update-slice.2 = bf16[128,86118]{1,0:T(8,128)(2,1)} dynamic-update-slice(bf16[128,86118]{1,0:T(8,128)(2,1)} %dynamic-update-slice.1, bf16[128,13824]{1,0:T(8,128)(2,1)} %copy.345, s32[]{} %constant.231, s32[]{} %constant.233) | dynamic-update-slice | bytes 7077892
  621.4 11.8 %dynamic-update-slice.3 = bf16[128,86118]{1,0:T(8,128)(2,1)} dynamic-update-slice(bf16[128,86118]{1,0:T(8,128)(2,1)} %dynamic-update-slice.2, bf16[128,4608]{1,0:T(8,128)(2,1)} %convert_element_type.822, s32[]{} %constant.231, s32[]{} %constant.234) | dynamic-update-slice | bytes 2359300
  634.9 21.1 %dynamic-update-slice.5 = bf16[128,86118]{1,0:T(8,128)(2,1)} dynamic-update-slice(bf16[128,86118]{1,0:T(8,128)(2,1)} %dynamic-update-slice.4, bf16[128,13824]{1,0:T(8,128)(2,1)S(1)} %copy-done.5, s32[]{} %constant.231, s32[]{} %constant.236) | dynamic-update-slice | bytes 7077892
  656.0 11.8 %dynamic-update-slice.6 = bf16[128,86118]{1,0:T(8,128)(2,1)} dynamic-update-slice(bf16[128,86118]{1,0:T(8,128)(2,1)} %dynamic-update-slice.5, bf16[128,4608]{1,0:T(8,128)(2,1)} %convert_element_type.831, s32[]{} %constant.231, s32[]{} %constant.237) | dynamic-update-slice | bytes 2359300
  669.5 32.4 %dynamic-update-slice.8 = bf16[128,86118]{1,0:T(8,128)(2,1)} dynamic-update-slice(bf16[128,86118]{1,0:T(8,128)(2,1)} %dynamic-update-slice.7, bf16[128,18432]{1,0:T(8,128)(2,1)} %convert_element_type.838, s32[]{} %constant.231, s32[]{} %constant.239) | dynamic-update-slice | bytes 9437188
  703.5 32.5 %dynamic-update-slice.10 = bf16[128,86118]{1,0:T(8,128)(2,1)} dynamic-update-slice(bf16[128,86118]{1,0:T(8,128)(2,1)} %dynamic-update-slice.9, bf16[128,18432]{1,0:T(8,128)(2,1)} %convert_element_type.842, s32[]{} %constant.231, s32[]{} %constant.241) | dynamic-update-slice | bytes 9437188
  737.7 20.9 %dynamic-update-slice.12 = bf16[128,86118]{1,0:T(8,128)(2,1)} dynamic-update-slice(bf16[128,86118]{1,0:T(8,128)(2,1)} %dynamic-update-slice.11, bf16[128,12288]{1,0:T(8,128)(2,1)S(1)} %copy-done.9, s32[]{} %constant.231, s32[]{} %constant.243) | dynamic-update-slice | bytes 6291460 | tf_op jit(solution)/shard_map/concatenate | solution.py:82
  758.7 21.1 %pad_bitcast_fusion = bf16[16,8,696,128]{3,1,2,0:T(8,128)(2,1)} fusion(bf16[128,86118]{1,0:T(8,128)(2,1)} %dynamic-update-slice.12), kind=kLoop, calls=%fused_computation.5 | loop fusion | bytes 44852736
  779.8 13.2 %copy.403 = bf16[16,8,696,128]{3,2,1,0:T(8,128)(2,1)S(1)} copy(bf16[16,8,696,128]{3,1,2,0:T(8,128)(2,1)} %pad_bitcast_fusion) | data formatting | bytes 45613056
  792.9 7.4 dynamic-slice_bitcast_fusion
  804.3 17.5 %collective-permute-done = bf16[4,4,4,696,128]{4,3,2,1,0:T(8,128)(2,1)} collective-permute-done((bf16[4,4,4,696,128]{4,3,2,1,0:T(8,128)(2,1)}, bf16[4,4,4,696,128]{4,3,2,1,0:T(8,128)(2,1)}, u32[]{:S(2)}, u32[]{:S(2)}) %collective-permute-start) | collective-permute-done | bytes 11403296 | tf_op jit(solution)/shard_map/ppermute | solution.py:65
  821.8 9.4 fusion.3
  868.4 5.8 add_convert_fusion.1
  925.3 10.4 %slice.218 = bf16[14848,6]{1,0:T(8,128)(2,1)} reshape(bf16[696,128]{1,0:T(8,128)(2,1)S(1)} %get-tuple-element.89) | data formatting | bytes 356352 | tf_op jit(solution)/shard_map/slice | solution.py:91
  (459 shorter events, 430.4 us)
Async XLA Ops:
  7.2 104.4 %all-gather.2.cloned.1.call-start = ((), (), s32[]{:S(2)}) async-start(), calls=%async_computation | async-start | bytes 22456320 | tf_op jit(solution)/shard_map/all_gather | solution.py:28
  157.5 35.5 %copy-start.35 = (f32[8,768]{1,0:T(8,128)}, f32[8,768]{1,0:T(8,128)S(1)}, u32[]{:S(2)}) copy-start(f32[8,768]{1,0:T(8,128)S(1)} %dynamic-slice_convert_fusion.1) | copy-start | bytes 73732
  158.4 34.6 %copy-start.10 = (f32[64,768]{1,0:T(8,128)}, f32[64,768]{1,0:T(8,128)S(1)}, u32[]{:S(2)}) copy-start(f32[64,768]{1,0:T(8,128)S(1)} %dynamic-slice_convert_fusion) | copy-start | bytes 589828
  599.0 35.9 %copy-start.5 = (bf16[128,13824]{1,0:T(8,128)(2,1)S(1)}, bf16[128,13824]{1,0:T(8,128)(2,1)}, u32[]{:S(2)}) copy-start(bf16[128,13824]{1,0:T(8,128)(2,1)} %copy.347) | copy-start | bytes 10616836
  804.0 17.8 %collective-permute-start = (bf16[4,4,4,696,128]{4,3,2,1,0:T(8,128)(2,1)}, bf16[4,4,4,696,128]{4,3,2,1,0:T(8,128)(2,1)}, u32[]{:S(2)}, u32[]{:S(2)}) collective-permute-start(bf16[4,4,4,696,128]{4,3,2,1,0:T(8,128)(2,1)} %dynamic-slice_bitcast_fusion), channel_id=1, source_target_pairs={{0,1},{1,0},{2,3},{3,2},{4,5},{5,4},{6,7},{7,6},{8,9},{9,8},{10,11... | collective-permute-start | bytes 34209800 | tf_op jit(solution)/shard_map/ppermute | solution.py:65
  837.0 16.4 %collective-permute-start.2 = (bf16[4,4,232,128]{3,2,1,0:T(8,128)(2,1)S(1)}, bf16[4,4,232,128]{3,2,1,0:T(8,128)(2,1)S(1)}, u32[]{:S(2)}, u32[]{:S(2)}) collective-permute-start(bf16[4,4,232,128]{3,2,1,0:T(8,128)(2,1)S(1)} %get-tuple-element.56), channel_id=1, source_target_pairs={{0,2},{1,7},{2,4},{3,1},{4,6},{5,3},{6,0},{7,5},{8,10},{9,15},{10,... | collective-permute-start | bytes 2850824 | tf_op jit(solution)/shard_map/ppermute | solution.py:50
  841.4 19.6 %collective-permute-start.20 = (bf16[4,4,232,128]{3,2,1,0:T(8,128)(2,1)}, bf16[4,4,232,128]{3,2,1,0:T(8,128)(2,1)}, u32[]{:S(2)}, u32[]{:S(2)}) collective-permute-start(bf16[4,4,232,128]{3,2,1,0:T(8,128)(2,1)} %get-tuple-element.60), channel_id=1, source_target_pairs={{0,8},{1,25},{8,16},{9,1},{16,24},{17,9},{24,0},{25,17},{2,10},{3,... | collective-permute-start | bytes 2850824 | tf_op jit(solution)/shard_map/ppermute | solution.py:50
  844.3 21.2 %collective-permute-start.11 = (bf16[4,4,232,128]{3,2,1,0:T(8,128)(2,1)}, bf16[4,4,232,128]{3,2,1,0:T(8,128)(2,1)}, u32[]{:S(2)}, u32[]{:S(2)}) collective-permute-start(bf16[4,4,232,128]{3,2,1,0:T(8,128)(2,1)} %get-tuple-element.58), channel_id=1, source_target_pairs={{0,32},{1,97},{32,64},{33,1},{64,96},{65,33},{96,0},{97,65},{2,34}... | collective-permute-start | bytes 2850824 | tf_op jit(solution)/shard_map/ppermute | solution.py:50
  845.0 22.1 %collective-permute-start.1 = (bf16[4,4,232,128]{3,2,1,0:T(8,128)(2,1)S(1)}, bf16[4,4,232,128]{3,2,1,0:T(8,128)(2,1)}, u32[]{:S(2)}, u32[]{:S(2)}) collective-permute-start(bf16[4,4,232,128]{3,2,1,0:T(8,128)(2,1)S(1)} %get-tuple-element.55), channel_id=1, source_target_pairs={{0,6},{1,3},{2,0},{3,5},{4,2},{5,7},{6,4},{7,1},{8,14},{9,11},{10,... | collective-permute-start | bytes 2850824 | tf_op jit(solution)/shard_map/ppermute | solution.py:50
  848.4 30.7 %collective-permute-start.19 = (bf16[4,4,232,128]{3,2,1,0:T(8,128)(2,1)}, bf16[4,4,232,128]{3,2,1,0:T(8,128)(2,1)S(1)}, u32[]{:S(2)}, u32[]{:S(2)}) collective-permute-start(bf16[4,4,232,128]{3,2,1,0:T(8,128)(2,1)} %get-tuple-element.59), channel_id=1, source_target_pairs={{0,24},{1,9},{8,0},{9,17},{16,8},{17,25},{24,16},{25,1},{2,26},{3,... | collective-permute-start | bytes 2850824 | tf_op jit(solution)/shard_map/ppermute | solution.py:50
  853.4 30.7 %collective-permute-start.10 = (bf16[4,4,232,128]{3,2,1,0:T(8,128)(2,1)}, bf16[4,4,232,128]{3,2,1,0:T(8,128)(2,1)S(1)}, u32[]{:S(2)}, u32[]{:S(2)}) collective-permute-start(bf16[4,4,232,128]{3,2,1,0:T(8,128)(2,1)} %get-tuple-element.57), channel_id=1, source_target_pairs={{0,96},{1,33},{32,0},{33,65},{64,32},{65,97},{96,64},{97,1},{2,98}... | collective-permute-start | bytes 2850824 | tf_op jit(solution)/shard_map/ppermute | solution.py:50
  860.9 15.0 %collective-permute-start.3 = (bf16[4,4,232,128]{3,2,1,0:T(8,128)(2,1)S(1)}, bf16[4,4,232,128]{3,2,1,0:T(8,128)(2,1)S(1)}, u32[]{:S(2)}, u32[]{:S(2)}) collective-permute-start(bf16[4,4,232,128]{3,2,1,0:T(8,128)(2,1)S(1)} %fusion.26), channel_id=1, source_target_pairs={{0,2},{1,7},{2,4},{3,1},{4,6},{5,3},{6,0},{7,5},{8,10},{9,15},{10,... | collective-permute-start | bytes 2850824 | tf_op jit(solution)/shard_map/ppermute | solution.py:50
  865.5 15.6 %collective-permute-start.21 = (bf16[4,4,232,128]{3,2,1,0:T(8,128)(2,1)S(1)}, bf16[4,4,232,128]{3,2,1,0:T(8,128)(2,1)S(1)}, u32[]{:S(2)}, u32[]{:S(2)}) collective-permute-start(bf16[4,4,232,128]{3,2,1,0:T(8,128)(2,1)S(1)} %fusion.20), channel_id=1, source_target_pairs={{0,8},{1,25},{8,16},{9,1},{16,24},{17,9},{24,0},{25,17},{2,10},{3,... | collective-permute-start | bytes 2850824 | tf_op jit(solution)/shard_map/ppermute | solution.py:50
  867.1 17.7 %collective-permute-start.12 = (bf16[4,4,232,128]{3,2,1,0:T(8,128)(2,1)S(1)}, bf16[4,4,232,128]{3,2,1,0:T(8,128)(2,1)S(1)}, u32[]{:S(2)}, u32[]{:S(2)}) collective-permute-start(bf16[4,4,232,128]{3,2,1,0:T(8,128)(2,1)S(1)} %fusion.23), channel_id=1, source_target_pairs={{0,32},{1,97},{32,64},{33,1},{64,96},{65,33},{96,0},{97,65},{2,34}... | collective-permute-start | bytes 2850824 | tf_op jit(solution)/shard_map/ppermute | solution.py:50
  877.8 18.0 %collective-permute-start.4 = (bf16[4,232,128]{2,1,0:T(8,128)(2,1)S(1)}, bf16[4,232,128]{2,1,0:T(8,128)(2,1)S(1)}, u32[]{:S(2)}, u32[]{:S(2)}) collective-permute-start(bf16[4,232,128]{2,1,0:T(8,128)(2,1)S(1)} %get-tuple-element.70), channel_id=1, source_target_pairs={{0,96},{1,33},{32,0},{33,65},{64,32},{65,97},{96,64},{97,1},{2,98}... | collective-permute-start | bytes 712712 | tf_op jit(solution)/shard_map/ppermute | solution.py:50
  879.1 8.0 collective-permute-start.5
  882.8 16.6 %collective-permute-start.22 = (bf16[4,232,128]{2,1,0:T(8,128)(2,1)S(1)}, bf16[4,232,128]{2,1,0:T(8,128)(2,1)S(1)}, u32[]{:S(2)}, u32[]{:S(2)}) collective-permute-start(bf16[4,232,128]{2,1,0:T(8,128)(2,1)S(1)} %get-tuple-element.74), channel_id=1, source_target_pairs={{0,6},{1,3},{2,0},{3,5},{4,2},{5,7},{6,4},{7,1},{8,14},{9,11},{10,... | collective-permute-start | bytes 712712 | tf_op jit(solution)/shard_map/ppermute | solution.py:50
  884.2 7.3 collective-permute-start.23
  885.3 17.8 %collective-permute-start.13 = (bf16[4,232,128]{2,1,0:T(8,128)(2,1)S(1)}, bf16[4,232,128]{2,1,0:T(8,128)(2,1)S(1)}, u32[]{:S(2)}, u32[]{:S(2)}) collective-permute-start(bf16[4,232,128]{2,1,0:T(8,128)(2,1)S(1)} %get-tuple-element.72), channel_id=1, source_target_pairs={{0,24},{1,9},{8,0},{9,17},{16,8},{17,25},{24,16},{25,1},{2,26},{3,... | collective-permute-start | bytes 712712 | tf_op jit(solution)/shard_map/ppermute | solution.py:50
  887.1 7.3 collective-permute-start.14
  891.5 6.1 collective-permute-start.6
  894.4 7.3 collective-permute-start.24
  895.8 9.4 collective-permute-start.15
  897.7 16.1 %collective-permute-start.7 = (bf16[232,128]{1,0:T(8,128)(2,1)S(1)}, bf16[232,128]{1,0:T(8,128)(2,1)S(1)}, u32[]{:S(2)}, u32[]{:S(2)}) collective-permute-start(bf16[232,128]{1,0:T(8,128)(2,1)S(1)} %get-tuple-element.76), channel_id=1, source_target_pairs={{0,24},{1,9},{8,0},{9,17},{16,8},{17,25},{24,16},{25,1},{2,26},{3,... | collective-permute-start | bytes 178184 | tf_op jit(solution)/shard_map/ppermute | solution.py:50
  899.4 6.8 collective-permute-start.8
  901.9 12.0 %collective-permute-start.25 = (bf16[232,128]{1,0:T(8,128)(2,1)S(1)}, bf16[232,128]{1,0:T(8,128)(2,1)S(1)}, u32[]{:S(2)}, u32[]{:S(2)}) collective-permute-start(bf16[232,128]{1,0:T(8,128)(2,1)S(1)} %get-tuple-element.80), channel_id=1, source_target_pairs={{0,96},{1,33},{32,0},{33,65},{64,32},{65,97},{96,64},{97,1},{2,98}... | collective-permute-start | bytes 178184 | tf_op jit(solution)/shard_map/ppermute | solution.py:50
  903.1 4.3 collective-permute-start.26
  905.3 10.7 %collective-permute-start.16 = (bf16[232,128]{1,0:T(8,128)(2,1)S(1)}, bf16[232,128]{1,0:T(8,128)(2,1)S(1)}, u32[]{:S(2)}, u32[]{:S(2)}) collective-permute-start(bf16[232,128]{1,0:T(8,128)(2,1)S(1)} %get-tuple-element.78), channel_id=1, source_target_pairs={{0,6},{1,3},{2,0},{3,5},{4,2},{5,7},{6,4},{7,1},{8,14},{9,11},{10,... | collective-permute-start | bytes 178184 | tf_op jit(solution)/shard_map/ppermute | solution.py:50
  906.2 5.4 collective-permute-start.17
  907.5 6.4 collective-permute-start.9
  911.6 4.4 collective-permute-start.27
  913.8 5.5 collective-permute-start.18
  (59 other events, 410.0 us)
Sparse Core Ops, SparseCore 0:
  20.5 91.0 all-gather.1
